TPU v7x, 32 devices: a whole 2x2x4 slice. The times are simulated.
32 devices in a mesh: sub: 16 (over z, y, core), strip: 2 (over x).
Axes of the slice: x: 2, y: 2, z: 4, core: 2. Of those that a mesh axis runs over, the one named last changes fastest.
Arguments:
- spectra: bfloat16 [32, 256, 2048], P('sub', 'strip'), may hold values from -6 to 6
- offsets: int32 [32], P('sub'), may hold values from 0 to 1023
Outputs:
- foreground: float32 [1024, 256, 32], P('strip', 'sub')
All inputs are finite; a program needn't handle non-finite values.
Results may differ from a plain program's by a relative error of at most 0.0068.
Values may be sent and summed in bfloat16 or wider, within the bound.
A program may use at most 64 MiB of HBM per device.

v0:
```python
import functools
import math

import jax
import jax.numpy as jnp
import numpy as np
from jax import lax
from jax.experimental import pallas as pl
from jax.experimental.pallas import tpu as pltpu
from jax.sharding import PartitionSpec as P

KR = 256
ROWS = 1024
COLS = 256
WIN = 8
BG = 16


def column_table(samples, parts):
    wide = COLS // parts + 2
    column = (np.arange(parts) * (wide - 2))[:, None] + np.arange(-1, wide - 1)[None, :]
    inside = (column >= 0) & (column < COLS)
    phase = ((np.arange(samples)[:, None, None] * column[None]) % samples) * (2.0 * math.pi / samples)
    cosine = np.where(inside, np.cos(phase), 0.0) / math.sqrt(samples)
    sine = np.where(inside, -np.sin(phase), 0.0) / math.sqrt(samples)
    upper = np.stack([cosine, sine], axis=2)
    lower = np.stack([-sine, cosine], axis=2)
    return jnp.asarray(np.concatenate([upper, lower], axis=0).astype(np.float32)).astype(jnp.bfloat16)


def row_table(rows):
    sample = jnp.arange(KR, dtype=jnp.int32)[:, None] - KR // 2
    phase = jnp.mod(rows[None, :] * sample, ROWS).astype(jnp.float32) * (2.0 * math.pi / ROWS)
    scale = jnp.where((rows >= 0) & (rows < ROWS), 1.0 / math.sqrt(KR), 0.0)[None, :]
    cosine = jnp.cos(phase) * scale
    sine = jnp.sin(phase) * scale
    upper = jnp.stack([cosine, sine], axis=1)
    lower = jnp.stack([-sine, cosine], axis=1)
    return jnp.concatenate([upper, lower], axis=0).astype(jnp.bfloat16)


def rotation(offsets, samples):
    angle = jnp.mod(offsets[:, None] * (samples[None, :] - KR // 2), ROWS).astype(jnp.float32) * (2.0 * math.pi / ROWS)
    return jnp.cos(angle), jnp.sin(angle)


def plain_body(spectra, offsets):
    own, depth = spectra.shape[:2]
    parts, strips = lax.axis_size("sub"), lax.axis_size("strip")
    wide = COLS // parts + 2
    high = ROWS // strips
    strip = lax.axis_index("strip")
    frames = own * parts
    table = column_table(spectra.shape[2] // 2, parts)
    cosine, sine = rotation(offsets, strip * depth + jnp.arange(depth, dtype=jnp.int32))
    mixed = jnp.einsum("skc,cdpn->dspnk", spectra, table, preferred_element_type=jnp.float32)
    real, imag = mixed[:, :, 0], mixed[:, :, 1]
    cosine, sine = cosine[None, :, None, :], sine[None, :, None, :]
    shifted = jnp.stack([real * cosine - imag * sine, real * sine + imag * cosine], axis=2).astype(jnp.bfloat16)
    held = lax.all_to_all(shifted, "sub", split_axis=0, concat_axis=0, tiled=True)
    held = held.reshape(frames, 2, wide, depth)
    whole = jnp.zeros((frames, 2, wide, strips, depth), jnp.bfloat16)
    for step in range(strips):
        part = held
        if step:
            part = lax.ppermute(held, "strip", [(i, (i + step) % strips) for i in range(strips)])
        source = jnp.mod(strip - step, strips)
        whole = lax.dynamic_update_slice(whole, part[:, :, :, None], (0, 0, 0, source, 0))
    wider = whole.reshape(frames, 2, wide, KR).astype(jnp.float32)
    summed = wider
    for lead in range(1, WIN):
        summed = summed + jnp.roll(wider, -lead, axis=0)
    rows = strip * high + jnp.arange(-1, high + 1, dtype=jnp.int32)
    product = jnp.einsum(
        "fpnk,pkqm->qnfm",
        summed.astype(jnp.bfloat16),
        row_table(rows).reshape(2, KR, 2, high + 2),
        preferred_element_type=jnp.float32,
    )
    log_power = jnp.log(1.0 + product[0] * product[0] + product[1] * product[1])
    total = log_power[:, :, :-2] + log_power[:, :, 1:-1] + log_power[:, :, 2:]
    filtered = (total[:-2] + total[1:-1] + total[2:]) / 9.0
    background = filtered
    for behind in range(1, BG):
        background = background + jnp.roll(filtered, behind, axis=1)
    return jnp.transpose(filtered - background / BG, (2, 0, 1))


LANES = 128
GROUP = 4
MESH = pl.DeviceIdType.MESH


def column_planes(samples):
    phase = (np.arange(COLS)[:, None] * np.arange(samples)[None, :] % samples) * (2.0 * math.pi / samples)
    planes = np.stack([np.cos(phase), -np.sin(phase)]) / math.sqrt(samples)
    return jnp.asarray(planes.astype(np.float32).astype(jnp.bfloat16))


def row_planes(high):
    row = np.concatenate([np.arange(high + LANES - 1), [-1]])
    used = (row <= high)[None, :]
    sample = np.arange(KR)[:, None] - KR // 2
    phase = (row[None, :] * sample % ROWS) * (2.0 * math.pi / ROWS)
    planes = np.stack([np.cos(phase) * used, np.sin(phase) * used]) / math.sqrt(KR)
    return jnp.asarray(planes.astype(np.float32).astype(jnp.bfloat16))


def frame_weights(width, sources, rows):
    frames = 2 * sources
    weights = np.zeros((width, frames, rows), np.float32)
    target = np.arange(frames)

    def place(at, column, frame):
        series = np.where(target == frame, 1.0, 0.0) - np.where((target - frame) % frames < BG, 1.0 / BG, 0.0)
        for near in range(max(column - 1, 0), min(column + 2, width)):
            weights[near, :, at] = series

    for lane in range(2):
        for source in range(sources):
            frame = 2 * source + lane
            for column in range(width):
                place((lane * sources + source) * width + column, column, frame)
            for side in range(2):
                place(2 * sources * width + (lane * sources + source) * 2 + side, (-1, width)[side], frame)
    return jnp.asarray(weights.reshape(width * frames, rows).astype(jnp.bfloat16))


def send_order(layers, group):
    order = [(0, place) for place in range(1, group)]
    half = layers // 2
    turn = [half] + [layer for away in range(half - 1, 0, -1) for layer in (half - away, half + away)]
    return order + [(layer, place) for place in range(group) for layer in turn[1:]] + [(half, place) for place in range(group)]


def product_of(a, b):
    return lax.dot_general(a, b, (((1,), (0,)), ((), ())), preferred_element_type=jnp.float32)


def product_t(a, b):
    return lax.dot_general(a, b, (((1,), (1,)), ((), ())), preferred_element_type=jnp.float32)


def ahead(value, steps):
    return jnp.concatenate([value[steps:], value[:steps]], axis=0)


def kernel(
    parts, strips, offsets_hbm, spectra_hbm, columns_hbm, rows_hbm, weights_hbm, out_ref,
    offsets_ref, spectra, columns, rows, weights, real, imag, edge, main, held, lhs, boxed, level,
    load_sem, own_sem, send_sem, recv_sem, pass_sem, got_sem,
):
    me, strip = lax.axis_index("sub"), lax.axis_index("strip")
    width = COLS // parts
    depth = spectra.shape[1]
    samples = spectra.shape[2] // 2
    high = out_ref.shape[2]
    other = 1 - strip

    loads = [
        pltpu.make_async_copy(source, target, load_sem.at[i])
        for i, (source, target) in enumerate(
            [(offsets_hbm, offsets_ref), (spectra_hbm, spectra), (columns_hbm, columns), (rows_hbm, rows), (weights_hbm, weights)]
        )
    ]
    for load in loads[:3]:
        load.start()
    barrier = pltpu.get_barrier_semaphore()
    for away in range(1, parts):
        pl.semaphore_signal(barrier, inc=1, device_id=(lax.rem(me + away, parts), strip), device_id_type=MESH)
    pl.semaphore_signal(barrier, inc=1, device_id=(me, other), device_id_type=MESH)

    loads[0].wait()
    lane = lax.broadcasted_iota(jnp.int32, (1, 2 * depth), 1)
    sample = strip * depth + jnp.where(lane < depth, lane, lane - depth) - KR // 2
    offset = jnp.where(lane < depth, offsets_ref[0], offsets_ref[1])
    angle = jnp.bitwise_and(offset * sample, ROWS - 1).astype(jnp.float32) * (2.0 * math.pi / ROWS)
    cosine, sine = jnp.cos(angle), jnp.sin(angle)
    edge[...] = jnp.zeros_like(edge)
    loads[1].wait()
    loads[2].wait()
    for load in loads[3:]:
        load.start()
    data = spectra[...].reshape(2 * depth, 2 * samples)
    data_re, data_im = data[:, :samples], data[:, samples:]
    step = COLS
    for at in range(0, COLS, step):
        cos_part, sin_part = columns[0, at : at + step], columns[1, at : at + step]
        re = product_t(cos_part, data_re) - product_t(sin_part, data_im)
        im = product_t(sin_part, data_re) + product_t(cos_part, data_im)
        first = at // width
        for part, value, ref in ((0, re * cosine - im * sine, real), (1, re * sine + im * cosine, imag)):
            ref[at : at + step] = value
            blocks = value.reshape(step // width, width // 4, 4, 2 * depth).astype(jnp.bfloat16)
            for own in range(2):
                main[
                    first : first + step // width, own * width // 4 : (own + 1) * width // 4, :, part * depth : (part + 1) * depth
                ] = blocks[:, :, :, own * depth : (own + 1) * depth]
    for part, ref in ((0, real), (1, imag)):
        for own in range(2):
            lanes, into = slice(own * depth, (own + 1) * depth), slice(part * depth, (part + 1) * depth)
            for d in range(parts):
                if d > 0:
                    edge[d, 2 * own : 2 * own + 1, into] = ref[d * width - 1 : d * width, lanes]
                if d < parts - 1:
                    edge[d, 2 * own + 1 : 2 * own + 2, into] = ref[(d + 1) * width : (d + 1) * width + 1, lanes]
    main[:, 2 * width // 4] = edge[:, :4].astype(jnp.bfloat16)

    pl.semaphore_wait(barrier, parts)

    def sends(to, where):
        return [
            pltpu.make_async_remote_copy(
                src_ref=source.at[to], dst_ref=target.at[strip, where], send_sem=send_sem.at[kind, to],
                recv_sem=recv_sem.at[kind, where], device_id=(to, strip), device_id_type=MESH,
            )
            for kind, source, target in ((0, main, held),)
        ]

    def passes(h, source, own=False):
        return [
            pltpu.make_async_remote_copy(
                src_ref=block.at[source] if own else target.at[h, source], dst_ref=target.at[h, source],
                send_sem=pass_sem.at[kind, source], recv_sem=got_sem.at[kind, source],
                device_id=(me, other), device_id_type=MESH,
            )
            for kind, block, target in ((0, main, held),)
        ]

    layers = parts // GROUP
    order = send_order(layers, GROUP)

    def device_at(layer, place):
        return lax.rem(me // GROUP + layer, layers) * GROUP + lax.rem(lax.rem(me, GROUP) + place, GROUP)

    def device_from(layer, place):
        return device_at(layers - layer, GROUP - place)

    for away in order:
        for copy in sends(device_at(*away), me):
            copy.start()
    kept = [
        pltpu.make_async_copy(source.at[me], target.at[strip, me], own_sem.at[kind])
        for kind, source, target in ((0, main, held),)
    ]
    for copy in passes(strip, me, own=True) + kept:
        copy.start()
    for away in order:
        source = device_from(*away)
        for copy in sends(source, source):
            copy.wait_recv()
        for copy in passes(strip, source):
            copy.start()
    top = 2 * parts * width
    odd = lax.rem(lax.broadcasted_iota(jnp.int32, (1, 1, 2 * depth), 2), 2)
    sign = 1.0 - 2.0 * (odd * strip).astype(jnp.float32)
    row_at = lax.broadcasted_iota(jnp.int32, (parts, 8, 2 * depth), 1)
    def window(h):
        whole = held[h].astype(jnp.float32) * sign[None]
        block = whole[:, : 2 * width // 4].reshape(parts, 2 * width, 2 * depth)
        first, second = block[:, :width], block[:, width:]
        near = whole[:, 2 * width // 4]
        near = jnp.concatenate([near, jnp.zeros_like(near)], axis=1)
        near_second = jnp.concatenate([pltpu.roll(near[i], 6, 0)[None] for i in range(parts)], axis=0)
        for is_halo, one, two in ((False, first, second), (True, near, near_second)):
            pair = one + two
            double = pair + ahead(pair, 1)
            quad = double + ahead(double, 2)
            for own, frame in ((0, quad), (1, quad - one + ahead(one, WIN // 2))):
                if is_halo:
                    frame = jnp.where(row_at < 2, frame, 0.0)
                    packed = []
                    for group in range(parts // 4):
                        total = frame[4 * group]
                        for j in range(1, 4):
                            total = total + pltpu.roll(frame[4 * group + j], 2 * j, 0)
                        packed.append(total)
                    flat = jnp.concatenate(packed, axis=0).astype(jnp.bfloat16)
                    at, size = top + own * 2 * parts, 2 * parts
                else:
                    flat = frame.reshape(parts * width, 2 * depth).astype(jnp.bfloat16)
                    at, size = own * parts * width, parts * width
                for part in range(2):
                    lhs[at : at + size, pl.ds(pl.multiple_of(part * KR + h * depth, depth), depth)] = flat[
                        :, part * depth : (part + 1) * depth
                    ]

    for copy in kept:
        copy.wait()
    window(strip)
    for away in [(0, 0)] + order:
        for copy in passes(other, device_from(*away)):
            copy.wait_recv()
    window(other)
    loads[3].wait()
    total_rows = top + 4 * parts
    tail = lax.broadcasted_iota(jnp.int32, (1, high + LANES), 1)
    outside = ((tail == high) & (strip == strips - 1)) | ((tail == high + LANES - 1) & (strip == 0))
    inside = jnp.where(outside, 0.0, 1.0)
    chunk = total_rows // 3
    for at in range(0, total_rows, chunk):
        left_re, left_im = lhs[at : at + chunk, :KR], lhs[at : at + chunk, KR:]
        re = product_of(left_re, rows[0]) - product_of(left_im, rows[1])
        im = product_of(left_re, rows[1]) + product_of(left_im, rows[0])
        power = jnp.log(1.0 + re * re + im * im) * inside
        summed = power + pltpu.roll(power, 1, 1) + pltpu.roll(power, high + LANES - 1, 1)
        boxed[at : at + chunk] = summed[:, :high]

    frames = 2 * parts
    block = boxed[:top].reshape(frames, width, high)
    mean = jnp.sum(block, axis=0, keepdims=True) * (1.0 / frames)
    level[:top] = (block - mean).reshape(top, high).astype(jnp.bfloat16)
    near = boxed[top:total_rows].reshape(frames // 4, 8, high)
    mean = jnp.sum(near, axis=0) * (1.0 / frames)
    mean = mean + pltpu.roll(mean, 4, 0)
    mean = mean + pltpu.roll(mean, 2, 0)
    level[top:total_rows] = (near - mean[None]).reshape(total_rows - top, high).astype(jnp.bfloat16)
    level[total_rows:] = jnp.zeros((level.shape[0] - total_rows, high), jnp.bfloat16)
    loads[4].wait()
    for c in range(0, width, 4):
        piece = product_of(weights[c * frames : (c + 4) * frames], level[...])
        out_ref[c : c + 4] = (piece * (1.0 / 9.0)).reshape(4, frames, high)
    for away in order:
        for copy in sends(device_at(*away), me):
            copy.wait_send()
    for away in [(0, 0)] + order:
        for copy in passes(strip, device_from(*away), own=away == (0, 0)):
            copy.wait_send()


def kernel_body(spectra, offsets):
    parts, strips = lax.axis_size("sub"), lax.axis_size("strip")
    own, depth, both = spectra.shape
    width, high = COLS // parts, ROWS // strips
    frames = own * parts
    total_rows = frames * (width + 2)
    padded = -(-total_rows // LANES) * LANES
    bf16, f32 = jnp.bfloat16, jnp.float32
    operands = (offsets, spectra, column_planes(both // 2), row_planes(high), frame_weights(width, parts, padded))
    out = pl.pallas_call(
        functools.partial(kernel, parts, strips),
        out_shape=jax.ShapeDtypeStruct((width, frames, high), f32),
        in_specs=[pl.BlockSpec(memory_space=pltpu.HBM)] * 5,
        out_specs=pl.BlockSpec(memory_space=pltpu.VMEM),
        scratch_shapes=[pltpu.SMEM(offsets.shape, offsets.dtype)]
        + [pltpu.VMEM(operand.shape, operand.dtype) for operand in operands[1:]]
        + [
            pltpu.VMEM((COLS, 2 * depth), f32),
            pltpu.VMEM((COLS, 2 * depth), f32),
            pltpu.VMEM((parts, 8, 2 * depth), f32),
            pltpu.VMEM((parts, 2 * width // 4 + 1, 4, 2 * depth), bf16),
            pltpu.VMEM((strips, parts, 2 * width // 4 + 1, 4, 2 * depth), bf16),
            pltpu.VMEM((total_rows, 2 * KR), bf16),
            pltpu.VMEM((total_rows, high), f32),
            pltpu.VMEM((padded, high), bf16),
            pltpu.SemaphoreType.DMA((5,)),
            pltpu.SemaphoreType.DMA((1,)),
            pltpu.SemaphoreType.DMA((1, parts)),
            pltpu.SemaphoreType.DMA((1, parts)),
            pltpu.SemaphoreType.DMA((1, parts)),
            pltpu.SemaphoreType.DMA((1, parts)),
        ],
        compiler_params=pltpu.CompilerParams(collective_id=0, has_side_effects=True, vmem_limit_bytes=48 << 20),
        name="sar",
    )(*(pltpu.with_memory_space_constraint(operand, pltpu.HBM) for operand in operands))
    return jnp.transpose(out, (2, 0, 1))


def fits(mesh):
    parts, strips = mesh.shape["sub"], mesh.shape["strip"]
    return strips == 2 and KR // strips == LANES and COLS % parts == 0 and COLS // parts == 16 and parts % 4 == 0


def body(mesh, spectra, offsets):
    if fits(mesh) and spectra.shape[0] == 2:
        return kernel_body(spectra, offsets)
    return plain_body(spectra, offsets)


def solution(mesh):
    in_specs = (P("sub", "strip", None), P("sub"))
    out_specs = P("strip", "sub", None)
    return jax.shard_map(
        functools.partial(body, mesh), mesh=mesh, in_specs=in_specs, out_specs=out_specs, check_vma=False
    )
```

profile of v0, /device:TPU:0, one launch (start us, length us, event | category | flops | bytes accessed | tf_op | source)
XLA Modules:
  0.0 22.0 jit_solution(2814662575265935832)
XLA Ops:
  0.0 21.0 %sar.1 = f32[16,32,512]{2,1,0:T(8,128)S(1)} custom-call(s32[2]{0:T(128)} %offsets_hbm.1, bf16[2,128,2048]{2,1,0:T(8,128)(2,1)} %spectra_hbm.1, bf16[2,256,1024]{2,1,0:T(8,128)(2,1)} %constant.6.clone.columns_hbm, bf16[2,256,640]{2,1,0:T(8,128)(2,1)} %constant.7.clone.rows_hbm, bf16[512,640]{1,0:T(8,128)(2,1)} %constant.8.clone.weights_hbm), custom_call_target="tpu_custom_call" | custom-call | tf_op jit(solution)/shard_map/sar/pallas_call | solution.py:340
  21.0 1.0 %copy.7 = f32[512,16,32]{0,2,1:T(8,128)} copy(f32[512,16,32]{0,2,1:T(8,128)S(1)} %bitcast.1) | data formatting | bytes 2097152
where the time goes:
time: 22.2 us; the launch traced here: 22 us
  Pallas kernels  21 us (95%)
  local copies, waits for them, and re-layouts  0.97 us (4%)
    pallas_call x1, Pallas kernels, kernel_body(): pl.pallas_call(functools.partial(kernel, parts, strips), out_shape=jax.Sh...  21 us
    unnamed x1, local copies, waits for them, and re-layouts  0.97 us

commit v1 on v0

--- a/solution.py
+++ b/solution.py
@@ -126,13 +126,6 @@
     return jnp.asarray(weights.reshape(width * frames, rows).astype(jnp.bfloat16))
 
 
-def send_order(layers, group):
-    order = [(0, place) for place in range(1, group)]
-    half = layers // 2
-    turn = [half] + [layer for away in range(half - 1, 0, -1) for layer in (half - away, half + away)]
-    return order + [(layer, place) for place in range(group) for layer in turn[1:]] + [(half, place) for place in range(group)]
-
-
 def product_of(a, b):
     return lax.dot_general(a, b, (((1,), (0,)), ((), ())), preferred_element_type=jnp.float32)
 
@@ -156,6 +149,21 @@
     samples = spectra.shape[2] // 2
     high = out_ref.shape[2]
     other = 1 - strip
+    layers = parts // GROUP
+    reach = layers // 2
+    layer, place = me // GROUP, lax.rem(me, GROUP)
+    upper, within = layer // reach, lax.rem(layer, reach)
+
+    def device_at(half, step, turn):
+        return (half * reach + step) * GROUP + lax.rem(place + turn + GROUP, GROUP)
+
+    close = [device_at(upper, within, turn) for turn in range(1, GROUP)]
+    close += [
+        device_at(upper, lax.rem(within + step, reach), turn) for step in range(1, reach) for turn in range(GROUP)
+    ]
+    outward = [(1 - upper) * (reach - 1) + (2 * upper - 1) * step for step in range(reach)]
+    targets = [device_at(1 - upper, step, turn) for step in outward for turn in range(GROUP)]
+    origins = [device_at(1 - upper, step, -turn) for step in outward for turn in range(GROUP)]
 
     loads = [
         pltpu.make_async_copy(source, target, load_sem.at[i])
@@ -168,7 +176,8 @@
     barrier = pltpu.get_barrier_semaphore()
     for away in range(1, parts):
         pl.semaphore_signal(barrier, inc=1, device_id=(lax.rem(me + away, parts), strip), device_id_type=MESH)
-    pl.semaphore_signal(barrier, inc=1, device_id=(me, other), device_id_type=MESH)
+    for near in [me] + close:
+        pl.semaphore_signal(barrier, inc=1, device_id=(near, other), device_id_type=MESH)
 
     loads[0].wait()
     lane = lax.broadcasted_iota(jnp.int32, (1, 2 * depth), 1)
@@ -206,51 +215,44 @@
                     edge[d, 2 * own + 1 : 2 * own + 2, into] = ref[(d + 1) * width : (d + 1) * width + 1, lanes]
     main[:, 2 * width // 4] = edge[:, :4].astype(jnp.bfloat16)
 
-    pl.semaphore_wait(barrier, parts)
-
-    def sends(to, where):
-        return [
-            pltpu.make_async_remote_copy(
-                src_ref=source.at[to], dst_ref=target.at[strip, where], send_sem=send_sem.at[kind, to],
-                recv_sem=recv_sem.at[kind, where], device_id=(to, strip), device_id_type=MESH,
-            )
-            for kind, source, target in ((0, main, held),)
-        ]
-
-    def passes(h, source, own=False):
-        return [
-            pltpu.make_async_remote_copy(
-                src_ref=block.at[source] if own else target.at[h, source], dst_ref=target.at[h, source],
-                send_sem=pass_sem.at[kind, source], recv_sem=got_sem.at[kind, source],
-                device_id=(me, other), device_id_type=MESH,
-            )
-            for kind, block, target in ((0, main, held),)
-        ]
-
-    layers = parts // GROUP
-    order = send_order(layers, GROUP)
-
-    def device_at(layer, place):
-        return lax.rem(me // GROUP + layer, layers) * GROUP + lax.rem(lax.rem(me, GROUP) + place, GROUP)
-
-    def device_from(layer, place):
-        return device_at(layers - layer, GROUP - place)
-
-    for away in order:
-        for copy in sends(device_at(*away), me):
-            copy.start()
-    kept = [
-        pltpu.make_async_copy(source.at[me], target.at[strip, me], own_sem.at[kind])
-        for kind, source, target in ((0, main, held),)
-    ]
-    for copy in passes(strip, me, own=True) + kept:
-        copy.start()
-    for away in order:
-        source = device_from(*away)
-        for copy in sends(source, source):
-            copy.wait_recv()
-        for copy in passes(strip, source):
-            copy.start()
+    pl.semaphore_wait(barrier, parts + len(close))
+
+    def send(to):
+        return pltpu.make_async_remote_copy(
+            src_ref=main.at[to], dst_ref=held.at[strip, me], send_sem=send_sem.at[to],
+            recv_sem=recv_sem.at[me], device_id=(to, strip), device_id_type=MESH,
+        )
+
+    def arrival(h, source, sem):
+        return pltpu.make_async_remote_copy(
+            src_ref=main.at[source], dst_ref=held.at[h, source], send_sem=send_sem.at[source],
+            recv_sem=sem.at[source], device_id=(source, strip), device_id_type=MESH,
+        )
+
+    def cross(to):
+        return pltpu.make_async_remote_copy(
+            src_ref=main.at[to], dst_ref=held.at[strip, me], send_sem=pass_sem.at[to],
+            recv_sem=got_sem.at[me], device_id=(to, other), device_id_type=MESH,
+        )
+
+    def forward(source):
+        return pltpu.make_async_remote_copy(
+            src_ref=held.at[strip, source], dst_ref=held.at[strip, source], send_sem=pass_sem.at[source],
+            recv_sem=got_sem.at[source], device_id=(me, other), device_id_type=MESH,
+        )
+
+    for to, near in zip(targets, [me] + close):
+        send(to).start()
+        cross(near).start()
+    for to in close:
+        send(to).start()
+    kept = pltpu.make_async_copy(main.at[me], held.at[strip, me], own_sem.at[0])
+    kept.start()
+    for source in origins:
+        arrival(strip, source, recv_sem).wait_recv()
+        forward(source).start()
+    for source in close:
+        arrival(strip, source, recv_sem).wait_recv()
     top = 2 * parts * width
     odd = lax.rem(lax.broadcasted_iota(jnp.int32, (1, 1, 2 * depth), 2), 2)
     sign = 1.0 - 2.0 * (odd * strip).astype(jnp.float32)
@@ -285,12 +287,10 @@
                         :, part * depth : (part + 1) * depth
                     ]
 
-    for copy in kept:
-        copy.wait()
+    kept.wait()
     window(strip)
-    for away in [(0, 0)] + order:
-        for copy in passes(other, device_from(*away)):
-            copy.wait_recv()
+    for source in [me] + close + origins:
+        arrival(other, source, got_sem).wait_recv()
     window(other)
     loads[3].wait()
     total_rows = top + 4 * parts
@@ -320,12 +320,12 @@
     for c in range(0, width, 4):
         piece = product_of(weights[c * frames : (c + 4) * frames], level[...])
         out_ref[c : c + 4] = (piece * (1.0 / 9.0)).reshape(4, frames, high)
-    for away in order:
-        for copy in sends(device_at(*away), me):
-            copy.wait_send()
-    for away in [(0, 0)] + order:
-        for copy in passes(strip, device_from(*away), own=away == (0, 0)):
-            copy.wait_send()
+    for to in targets + close:
+        send(to).wait_send()
+    for to in [me] + close:
+        cross(to).wait_send()
+    for source in origins:
+        forward(source).wait_send()
 
 
 def kernel_body(spectra, offsets):
@@ -355,10 +355,10 @@
             pltpu.VMEM((padded, high), bf16),
             pltpu.SemaphoreType.DMA((5,)),
             pltpu.SemaphoreType.DMA((1,)),
-            pltpu.SemaphoreType.DMA((1, parts)),
-            pltpu.SemaphoreType.DMA((1, parts)),
-            pltpu.SemaphoreType.DMA((1, parts)),
-            pltpu.SemaphoreType.DMA((1, parts)),
+            pltpu.SemaphoreType.DMA((parts,)),
+            pltpu.SemaphoreType.DMA((parts,)),
+            pltpu.SemaphoreType.DMA((parts,)),
+            pltpu.SemaphoreType.DMA((parts,)),
         ],
         compiler_params=pltpu.CompilerParams(collective_id=0, has_side_effects=True, vmem_limit_bytes=48 << 20),
         name="sar",

time: 22.2 us -> 20.9 us (0.941)
  Pallas kernels: 21 us -> 19.7 us
    pallas_call x1, Pallas kernels: 21 us -> 19.7 us  [kernel_body(): pl.pallas_call(functools.partial(kernel, parts, strips), out_shape=jax.Sh...]
where the time goes in v1:
time: 20.9 us; the launch traced here: 20.7 us
  Pallas kernels  19.7 us (94%)
  local copies, waits for them, and re-layouts  0.97 us (5%)
    pallas_call x1, Pallas kernels, kernel_body(): pl.pallas_call(functools.partial(kernel, parts, strips), out_shape=jax.Sh...  19.7 us
    unnamed x1, local copies, waits for them, and re-layouts  0.97 us

profile of v1, /device:TPU:0, one launch (start us, length us, event | category | flops | bytes accessed | tf_op | source)
XLA Modules:
  0.0 20.7 jit_solution(1768254999225564554)
XLA Ops:
  0.0 19.7 %sar.1 = f32[16,32,512]{2,1,0:T(8,128)S(1)} custom-call(s32[2]{0:T(128)} %offsets_hbm.1, bf16[2,128,2048]{2,1,0:T(8,128)(2,1)} %spectra_hbm.1, bf16[2,256,1024]{2,1,0:T(8,128)(2,1)} %constant.6.clone.columns_hbm, bf16[2,256,640]{2,1,0:T(8,128)(2,1)} %constant.7.clone.rows_hbm, bf16[512,640]{1,0:T(8,128)(2,1)} %constant.8.clone.weights_hbm), custom_call_target="tpu_custom_call" | custom-call | tf_op jit(solution)/shard_map/sar/pallas_call | solution.py:340
  19.7 1.0 %copy.7 = f32[512,16,32]{0,2,1:T(8,128)} copy(f32[512,16,32]{0,2,1:T(8,128)S(1)} %bitcast.1) | data formatting | bytes 2097152

commit v2 on v1

v2 whole, which is shorter than its diff:
```python
import functools
import math

import jax
import jax.numpy as jnp
import numpy as np
from jax import lax
from jax.experimental import pallas as pl
from jax.experimental.pallas import tpu as pltpu
from jax.sharding import PartitionSpec as P

KR = 256
ROWS = 1024
COLS = 256
WIN = 8
BG = 16


def column_table(samples, parts):
    wide = COLS // parts + 2
    column = (np.arange(parts) * (wide - 2))[:, None] + np.arange(-1, wide - 1)[None, :]
    inside = (column >= 0) & (column < COLS)
    phase = ((np.arange(samples)[:, None, None] * column[None]) % samples) * (2.0 * math.pi / samples)
    cosine = np.where(inside, np.cos(phase), 0.0) / math.sqrt(samples)
    sine = np.where(inside, -np.sin(phase), 0.0) / math.sqrt(samples)
    upper = np.stack([cosine, sine], axis=2)
    lower = np.stack([-sine, cosine], axis=2)
    return jnp.asarray(np.concatenate([upper, lower], axis=0).astype(np.float32)).astype(jnp.bfloat16)


def row_table(rows):
    sample = jnp.arange(KR, dtype=jnp.int32)[:, None] - KR // 2
    phase = jnp.mod(rows[None, :] * sample, ROWS).astype(jnp.float32) * (2.0 * math.pi / ROWS)
    scale = jnp.where((rows >= 0) & (rows < ROWS), 1.0 / math.sqrt(KR), 0.0)[None, :]
    cosine = jnp.cos(phase) * scale
    sine = jnp.sin(phase) * scale
    upper = jnp.stack([cosine, sine], axis=1)
    lower = jnp.stack([-sine, cosine], axis=1)
    return jnp.concatenate([upper, lower], axis=0).astype(jnp.bfloat16)


def rotation(offsets, samples):
    angle = jnp.mod(offsets[:, None] * (samples[None, :] - KR // 2), ROWS).astype(jnp.float32) * (2.0 * math.pi / ROWS)
    return jnp.cos(angle), jnp.sin(angle)


def plain_body(spectra, offsets):
    own, depth = spectra.shape[:2]
    parts, strips = lax.axis_size("sub"), lax.axis_size("strip")
    wide = COLS // parts + 2
    high = ROWS // strips
    strip = lax.axis_index("strip")
    frames = own * parts
    table = column_table(spectra.shape[2] // 2, parts)
    cosine, sine = rotation(offsets, strip * depth + jnp.arange(depth, dtype=jnp.int32))
    mixed = jnp.einsum("skc,cdpn->dspnk", spectra, table, preferred_element_type=jnp.float32)
    real, imag = mixed[:, :, 0], mixed[:, :, 1]
    cosine, sine = cosine[None, :, None, :], sine[None, :, None, :]
    shifted = jnp.stack([real * cosine - imag * sine, real * sine + imag * cosine], axis=2).astype(jnp.bfloat16)
    held = lax.all_to_all(shifted, "sub", split_axis=0, concat_axis=0, tiled=True)
    held = held.reshape(frames, 2, wide, depth)
    whole = jnp.zeros((frames, 2, wide, strips, depth), jnp.bfloat16)
    for step in range(strips):
        part = held
        if step:
            part = lax.ppermute(held, "strip", [(i, (i + step) % strips) for i in range(strips)])
        source = jnp.mod(strip - step, strips)
        whole = lax.dynamic_update_slice(whole, part[:, :, :, None], (0, 0, 0, source, 0))
    wider = whole.reshape(frames, 2, wide, KR).astype(jnp.float32)
    summed = wider
    for lead in range(1, WIN):
        summed = summed + jnp.roll(wider, -lead, axis=0)
    rows = strip * high + jnp.arange(-1, high + 1, dtype=jnp.int32)
    product = jnp.einsum(
        "fpnk,pkqm->qnfm",
        summed.astype(jnp.bfloat16),
        row_table(rows).reshape(2, KR, 2, high + 2),
        preferred_element_type=jnp.float32,
    )
    log_power = jnp.log(1.0 + product[0] * product[0] + product[1] * product[1])
    total = log_power[:, :, :-2] + log_power[:, :, 1:-1] + log_power[:, :, 2:]
    filtered = (total[:-2] + total[1:-1] + total[2:]) / 9.0
    background = filtered
    for behind in range(1, BG):
        background = background + jnp.roll(filtered, behind, axis=1)
    return jnp.transpose(filtered - background / BG, (2, 0, 1))


LANES = 128
GROUP = 4
RADIX = 4
LAYERS = 4
MESH = pl.DeviceIdType.MESH


def column_planes(samples):
    phase = (np.arange(COLS)[:, None] * np.arange(samples // RADIX)[None, :] % samples) * (2.0 * math.pi / samples)
    cosine, sine = np.cos(phase) / math.sqrt(samples), -np.sin(phase) / math.sqrt(samples)
    planes = np.block([[[cosine, -sine]], [[sine, cosine]]])
    planes = planes.reshape(2, COLS // RADIX, RADIX, 2 * samples // RADIX).transpose(2, 0, 1, 3)
    planes = planes.reshape(RADIX, 2 * COLS // RADIX, 2 * samples // RADIX)
    return jnp.asarray(planes.astype(np.float32).astype(jnp.bfloat16))


def row_planes(high):
    row = np.concatenate([np.arange(high + LANES - 1), [-1]])
    used = (row <= high)[None, :]
    phase = (row[None, :] * (2 * np.arange(KR // 2)[:, None] + 1) % (2 * ROWS)) * (math.pi / ROWS)
    planes = np.concatenate([np.cos(phase) * used, -np.sin(phase) * used]) / math.sqrt(KR)
    return jnp.asarray(planes.astype(np.float32).astype(jnp.bfloat16))


def stages(upper):
    return [[2 * upper], [LAYERS - 1], [1 - upper, 2 - upper]]


def frame_weights(width, sources, rows):
    frames = 2 * sources
    weights = np.zeros((2, width, frames, rows), np.float32)
    target = np.arange(frames)

    def place(upper, at, column, frame):
        series = np.where(target == frame, 1.0, 0.0) - np.where((target - frame) % frames < BG, 1.0 / BG, 0.0)
        for near in range(max(column - 1, 0), min(column + 2, width)):
            weights[upper, near, :, at] = series

    for upper in range(2):
        at, edge_at = 0, frames * width
        for group in stages(upper):
            held = [layer * GROUP + index for layer in group for index in range(GROUP)]
            for lane in range(2):
                for source in held:
                    for spot in range(width):
                        place(upper, at, RADIX * (spot % (width // RADIX)) + spot // (width // RADIX), 2 * source + lane)
                        at += 1
            for lane in range(2):
                for source in held:
                    for side in range(2):
                        place(upper, edge_at, (-1, width)[side], 2 * source + lane)
                        edge_at += 1
    return jnp.asarray(weights.reshape(2, width * frames, rows).astype(jnp.bfloat16))


def product_of(a, b):
    return lax.dot_general(a, b, (((1,), (0,)), ((), ())), preferred_element_type=jnp.float32)


def product_t(a, b):
    return lax.dot_general(a, b, (((1,), (1,)), ((), ())), preferred_element_type=jnp.float32)


def kernel(
    parts, strips, offsets_hbm, spectra_hbm, columns_hbm, rows_hbm, weights_hbm, out_ref,
    offsets_ref, spectra, columns, rows, weights, mixed, ends, edge, main, held, lhs, boxed, level,
    load_sem, own_sem, send_sem, recv_sem, pass_sem, got_sem,
):
    me, strip = lax.axis_index("sub"), lax.axis_index("strip")
    width = COLS // parts
    depth = spectra.shape[1]
    samples = spectra.shape[2] // 2
    high = out_ref.shape[2]
    other = 1 - strip
    reach = LAYERS // 2
    layer, place = me // GROUP, lax.rem(me, GROUP)
    upper, within = layer // reach, lax.rem(layer, reach)

    def device_at(half, step, turn):
        return (half * reach + step) * GROUP + lax.rem(place + turn + GROUP, GROUP)

    close = [device_at(upper, within, turn) for turn in range(1, GROUP)]
    close += [
        device_at(upper, lax.rem(within + step, reach), turn) for step in range(1, reach) for turn in range(GROUP)
    ]
    outward = [(1 - upper) * (reach - 1) + (2 * upper - 1) * step for step in range(reach)]
    targets = [device_at(1 - upper, step, turn) for step in outward for turn in range(GROUP)]
    origins = [device_at(1 - upper, step, -turn) for step in outward for turn in range(GROUP)]

    def load(source, target, i):
        return pltpu.make_async_copy(source, target, load_sem.at[i])

    loads = [
        load(offsets_hbm, offsets_ref, 0),
        load(spectra_hbm.at[0], spectra.at[0], 1),
        load(spectra_hbm.at[1], spectra.at[1], 2),
        load(columns_hbm, columns, 3),
        load(rows_hbm, rows, 4),
        load(weights_hbm.at[upper], weights, 5),
    ]
    for copy in loads[:4]:
        copy.start()
    barrier = pltpu.get_barrier_semaphore()
    for away in range(1, parts):
        pl.semaphore_signal(barrier, inc=1, device_id=(lax.rem(me + away, parts), strip), device_id_type=MESH)
    for near in [me] + close:
        pl.semaphore_signal(barrier, inc=1, device_id=(near, other), device_id_type=MESH)

    loads[0].wait()
    lane = lax.broadcasted_iota(jnp.int32, (1, 2 * depth), 1)
    sample = strip * depth + jnp.where(lane < depth, lane, lane - depth) - KR // 2
    offset = jnp.where(lane < depth, offsets_ref[0], offsets_ref[1])
    angle = jnp.bitwise_and(offset * sample, ROWS - 1).astype(jnp.float32) * (2.0 * math.pi / ROWS)
    cosine, sine = jnp.cos(angle), jnp.sin(angle)
    edge[...] = jnp.zeros_like(edge)
    quarter = samples // RADIX
    for own in range(2):
        loads[1 + own].wait()
        re = [spectra[own, :, p * quarter : (p + 1) * quarter].astype(jnp.float32) for p in range(RADIX)]
        im = [spectra[own, :, samples + p * quarter : samples + (p + 1) * quarter].astype(jnp.float32) for p in range(RADIX)]
        even_re, even_im, gap_re, gap_im = re[0] + re[2], im[0] + im[2], re[0] - re[2], im[0] - im[2]
        odd_re, odd_im, turn_re, turn_im = re[1] + re[3], im[1] + im[3], im[1] - im[3], re[3] - re[1]
        folded = [
            (even_re + odd_re, even_im + odd_im), (gap_re + turn_re, gap_im + turn_im),
            (even_re - odd_re, even_im - odd_im), (gap_re - turn_re, gap_im - turn_im),
        ]
        for residue, pair in enumerate(folded):
            for part, value in enumerate(pair):
                mixed[residue, own * depth : (own + 1) * depth, part * quarter : (part + 1) * quarter] = value.astype(jnp.bfloat16)
    loads[3].wait()
    for copy in loads[4:]:
        copy.start()
    rank = COLS // RADIX
    slots = width // RADIX
    back = lax.broadcasted_iota(jnp.int32, (rank, depth), 1)
    back = (1 - strip) * (depth - 1 - 2 * back) + back
    for residue in range(RADIX):
        both = product_t(columns[residue], mixed[residue])
        re, im = both[:rank], both[rank:]
        for part, value in ((0, re * cosine - im * sine), (1, re * sine + im * cosine)):
            for own in range(2):
                turned = jnp.take_along_axis(value[:, own * depth : (own + 1) * depth], back, axis=1, mode="promise_in_bounds")
                into = slice(part * depth, (part + 1) * depth)
                if residue == 0:
                    ends[2 * own + 1, :, into] = turned
                if residue == RADIX - 1:
                    ends[2 * own, :, into] = turned
                main[:, own * RADIX + residue, :, into] = (
                    turned.reshape(parts, slots, depth).astype(jnp.bfloat16)
                )
    for own in range(2):
        for d in range(parts):
            if d > 0:
                edge[d, 2 * own : 2 * own + 1] = ends[2 * own, d * slots - 1 : d * slots]
            if d < parts - 1:
                edge[d, 2 * own + 1 : 2 * own + 2] = ends[2 * own + 1, (d + 1) * slots : (d + 1) * slots + 1]
    main[:, 2 * RADIX] = edge[:, :4].astype(jnp.bfloat16)

    pl.semaphore_wait(barrier, parts + len(close))

    def send(to):
        return pltpu.make_async_remote_copy(
            src_ref=main.at[to], dst_ref=held.at[strip, me], send_sem=send_sem.at[to],
            recv_sem=recv_sem.at[me], device_id=(to, strip), device_id_type=MESH,
        )

    def arrival(h, source, sem):
        return pltpu.make_async_remote_copy(
            src_ref=main.at[source], dst_ref=held.at[h, source], send_sem=send_sem.at[source],
            recv_sem=sem.at[source], device_id=(source, strip), device_id_type=MESH,
        )

    def cross(to):
        return pltpu.make_async_remote_copy(
            src_ref=main.at[to], dst_ref=held.at[strip, me], send_sem=pass_sem.at[to],
            recv_sem=got_sem.at[me], device_id=(to, other), device_id_type=MESH,
        )

    def forward(source):
        return pltpu.make_async_remote_copy(
            src_ref=held.at[strip, source], dst_ref=held.at[strip, source], send_sem=pass_sem.at[source],
            recv_sem=got_sem.at[source], device_id=(me, other), device_id_type=MESH,
        )

    for to, near in zip(targets, [me] + close):
        send(to).start()
        cross(near).start()
    for to in close:
        send(to).start()
    kept = pltpu.make_async_copy(main.at[me], held.at[strip, me], own_sem.at[0])
    kept.start()

    alternate = 1.0 - 2.0 * lax.rem(lax.broadcasted_iota(jnp.int32, (1, 1, 2 * depth), 2), 2).astype(jnp.float32)
    signs = [1.0 - strip * (1.0 + alternate), 1.0 - strip * (1.0 - alternate)]
    row_at = lax.broadcasted_iota(jnp.int32, (GROUP, 8, 2 * depth), 1)

    def window(h, first, count):
        block = []
        for step in range(count + 1):
            at = lax.rem(first + step, LAYERS) * GROUP
            block.append(held[h, pl.ds(at, GROUP)].astype(jnp.float32) * signs[h][None])
        whole = jnp.concatenate(block, axis=0)
        number = count * GROUP
        body = whole[:, : 2 * RADIX].reshape(number + GROUP, 2 * width, 2 * depth)
        near = whole[:, 2 * RADIX]
        near = jnp.concatenate([near, jnp.zeros_like(near)], axis=1)
        near_second = jnp.concatenate([pltpu.roll(near[i], 6, 0)[None] for i in range(number + GROUP)], axis=0)
        results = []
        for one, two in ((body[:, :width], body[:, width:]), (near, near_second)):
            pair = one + two
            double = pair[:-1] + pair[1:]
            quad = double[:number] + double[2 : number + 2]
            results.append((quad, quad - one[:number] + one[WIN // 2 : number + WIN // 2]))
        packed = []
        for frame in results[1]:
            for group in range(count):
                masked = jnp.where(row_at < 2, frame[GROUP * group : GROUP * (group + 1)], 0.0)
                total = masked[0]
                for j in range(1, GROUP):
                    total = total + pltpu.roll(masked[j], 2 * j, 0)
                packed.append(total)
        flat = [frame.reshape(number * width, 2 * depth) for frame in results[0]]
        return jnp.concatenate(flat + packed, axis=0)

    tail = lax.broadcasted_iota(jnp.int32, (1, high + LANES), 1)
    outside = ((tail == high) & (strip == strips - 1)) | ((tail == high + LANES - 1) & (strip == 0))
    inside = jnp.where(outside, 0.0, 1.0)

    def image(lower_half, upper_half):
        total = upper_half + lower_half
        gap = upper_half - lower_half
        size = total.shape[0]
        lhs[:size, :depth] = total[:, :depth].astype(jnp.bfloat16)
        lhs[:size, depth:] = gap[:, depth:].astype(jnp.bfloat16)
        lhs[size : 2 * size, :depth] = total[:, depth:].astype(jnp.bfloat16)
        lhs[size : 2 * size, depth:] = (-gap[:, :depth]).astype(jnp.bfloat16)
        step = size // 2
        pieces = []
        for at in range(0, size, step):
            re = product_of(lhs[at : at + step], rows[...])
            im = product_of(lhs[size + at : size + at + step], rows[...])
            power = jnp.log(1.0 + re * re + im * im) * inside
            pieces.append((power + pltpu.roll(power, 1, 1) + pltpu.roll(power, high + LANES - 1, 1))[:, :high])
        return pieces

    batch = GROUP * width
    for source in origins[:GROUP]:
        arrival(strip, source, recv_sem).wait_recv()
        forward(source).start()
    for source in close:
        arrival(strip, source, recv_sem).wait_recv()
    kept.wait()
    for source in [me] + close:
        arrival(other, source, got_sem).wait_recv()
    loads[4].wait()
    pieces = image(window(0, 2 * upper, 1), window(1, 2 * upper, 1))
    size = 2 * batch + 2 * 8
    for i, piece in enumerate(pieces):
        boxed[0, i * (size // 2) : (i + 1) * (size // 2)] = piece
    for source in origins[GROUP:]:
        arrival(strip, source, recv_sem).wait_recv()
        forward(source).start()
    for source in origins[:GROUP]:
        arrival(other, source, got_sem).wait_recv()
    pieces = image(window(0, LAYERS - 1, 1), window(1, LAYERS - 1, 1))
    for i, piece in enumerate(pieces):
        boxed[1, i * (size // 2) : (i + 1) * (size // 2)] = piece
    early = boxed[:, : 2 * batch].reshape(2, 2 * GROUP, width, high)
    mean = jnp.sum(jnp.sum(early, axis=0), axis=0) * (1.0 / (4 * GROUP))
    for i in range(2):
        level[2 * batch * i : 2 * batch * (i + 1)] = (early[i] - mean[None]).reshape(2 * batch, high).astype(jnp.bfloat16)
    early_near = boxed[:, 2 * batch : size].reshape(4, 8, high)
    near_mean = jnp.sum(early_near, axis=0) * (1.0 / (4 * GROUP))
    near_mean = near_mean + pltpu.roll(near_mean, 4, 0)
    near_mean = near_mean + pltpu.roll(near_mean, 2, 0)
    top = 2 * parts * width
    level[top : top + 32] = (early_near - near_mean[None]).reshape(32, high).astype(jnp.bfloat16)
    level[top + 64 :] = jnp.zeros((level.shape[0] - top - 64, high), jnp.bfloat16)

    for source in origins[GROUP:]:
        arrival(other, source, got_sem).wait_recv()
    pieces = image(window(0, 1 - upper, 2), window(1, 1 - upper, 2))
    late = jnp.concatenate(pieces, axis=0)
    block = late[: 4 * batch].reshape(4 * GROUP, width, high)
    level[4 * batch : 8 * batch] = (block - mean[None]).reshape(4 * batch, high).astype(jnp.bfloat16)
    near = late[4 * batch :].reshape(4, 8, high)
    level[top + 32 : top + 64] = (near - near_mean[None]).reshape(32, high).astype(jnp.bfloat16)
    loads[5].wait()
    frames = 2 * parts
    for c in range(0, width, 4):
        piece = product_of(weights[c * frames : (c + 4) * frames], level[...])
        out_ref[c : c + 4] = (piece * (1.0 / 9.0)).reshape(4, frames, high)
    for to in targets + close:
        send(to).wait_send()
    for to in [me] + close:
        cross(to).wait_send()
    for source in origins:
        forward(source).wait_send()


def kernel_body(spectra, offsets):
    parts, strips = lax.axis_size("sub"), lax.axis_size("strip")
    own, depth, both = spectra.shape
    width, high = COLS // parts, ROWS // strips
    frames = own * parts
    total_rows = frames * (width + 2)
    padded = -(-total_rows // LANES) * LANES
    bf16, f32 = jnp.bfloat16, jnp.float32
    operands = (offsets, spectra, column_planes(both // 2), row_planes(high), frame_weights(width, parts, padded))
    shapes = [operand.shape for operand in operands[1:4]] + [operands[4].shape[1:]]
    half = 2 * GROUP * width + 2 * 8
    out = pl.pallas_call(
        functools.partial(kernel, parts, strips),
        out_shape=jax.ShapeDtypeStruct((width, frames, high), f32),
        in_specs=[pl.BlockSpec(memory_space=pltpu.HBM)] * 5,
        out_specs=pl.BlockSpec(memory_space=pltpu.VMEM),
        scratch_shapes=[pltpu.SMEM(offsets.shape, offsets.dtype)]
        + [pltpu.VMEM(shape, bf16) for shape in shapes]
        + [
            pltpu.VMEM((RADIX, 2 * depth, both // RADIX), bf16),
            pltpu.VMEM((4, COLS // RADIX, 2 * depth), f32),
            pltpu.VMEM((parts, 8, 2 * depth), f32),
            pltpu.VMEM((parts, 2 * RADIX + 1, width // RADIX, 2 * depth), bf16),
            pltpu.VMEM((strips, parts, 2 * RADIX + 1, width // RADIX, 2 * depth), bf16),
            pltpu.VMEM((4 * half, KR), bf16),
            pltpu.VMEM((2, half, high), f32),
            pltpu.VMEM((padded, high), bf16),
            pltpu.SemaphoreType.DMA((6,)),
            pltpu.SemaphoreType.DMA((1,)),
            pltpu.SemaphoreType.DMA((parts,)),
            pltpu.SemaphoreType.DMA((parts,)),
            pltpu.SemaphoreType.DMA((parts,)),
            pltpu.SemaphoreType.DMA((parts,)),
        ],
        compiler_params=pltpu.CompilerParams(collective_id=0, has_side_effects=True, vmem_limit_bytes=48 << 20),
        name="sar",
    )(*(pltpu.with_memory_space_constraint(operand, pltpu.HBM) for operand in operands))
    return jnp.transpose(out, (2, 0, 1))


def fits(mesh):
    parts, strips = mesh.shape["sub"], mesh.shape["strip"]
    return strips == 2 and KR // strips == LANES and COLS % parts == 0 and COLS // parts == 16 and parts == LAYERS * GROUP


def body(mesh, spectra, offsets):
    if fits(mesh) and spectra.shape[0] == 2:
        return kernel_body(spectra, offsets)
    return plain_body(spectra, offsets)


def solution(mesh):
    in_specs = (P("sub", "strip", None), P("sub"))
    out_specs = P("strip", "sub", None)
    return jax.shard_map(
        functools.partial(body, mesh), mesh=mesh, in_specs=in_specs, out_specs=out_specs, check_vma=False
    )
```

time: 20.9 us -> 21.5 us (1.029)
  Pallas kernels: 19.7 us -> 20.3 us
    pallas_call x1, Pallas kernels: 19.7 us -> 20.3 us  [kernel_body(): pl.pallas_call(functools.partial(kernel, parts, strips), out_shape=jax.Sh...]
where the time goes in v2:
time: 21.5 us; the launch traced here: 21.3 us
  Pallas kernels  20.3 us (94%)
  local copies, waits for them, and re-layouts  0.97 us (5%)
    pallas_call x1, Pallas kernels, kernel_body(): pl.pallas_call(functools.partial(kernel, parts, strips), out_shape=jax.Sh...  20.3 us
    unnamed x1, local copies, waits for them, and re-layouts  0.97 us

profile of v2, /device:TPU:0, one launch (start us, length us, event | category | flops | bytes accessed | tf_op | source)
XLA Modules:
  0.0 21.3 jit_solution(11844789385604610267)
XLA Ops:
  0.0 20.3 %sar.1 = f32[16,32,512]{2,1,0:T(8,128)S(1)} custom-call(s32[2]{0:T(128)} %offsets_hbm.1, bf16[2,128,2048]{2,1,0:T(8,128)(2,1)} %spectra_hbm.1, bf16[4,128,512]{2,1,0:T(8,128)(2,1)} %constant.6.clone.columns_hbm, bf16[256,640]{1,0:T(8,128)(2,1)} %constant.7.clone.rows_hbm, bf16[2,512,640]{2,1,0:T(8,128)(2,1)} %constant.8.clone.weights_hbm), custom_call_target="tpu_custom_call" | custom-call | tf_op jit(solution)/shard_map/sar/pallas_call | solution.py:400
  20.3 1.0 %copy.7 = f32[512,16,32]{0,2,1:T(8,128)} copy(f32[512,16,32]{0,2,1:T(8,128)S(1)} %bitcast.1) | data formatting | bytes 2097152

commit v3 on v2

--- a/solution.py
+++ b/solution.py
@@ -332,7 +332,7 @@
         return pieces
 
     batch = GROUP * width
-    for source in origins[:GROUP]:
+    for source in origins:
         arrival(strip, source, recv_sem).wait_recv()
         forward(source).start()
     for source in close:
@@ -345,9 +345,6 @@
     size = 2 * batch + 2 * 8
     for i, piece in enumerate(pieces):
         boxed[0, i * (size // 2) : (i + 1) * (size // 2)] = piece
-    for source in origins[GROUP:]:
-        arrival(strip, source, recv_sem).wait_recv()
-        forward(source).start()
     for source in origins[:GROUP]:
         arrival(other, source, got_sem).wait_recv()
     pieces = image(window(0, LAYERS - 1, 1), window(1, LAYERS - 1, 1))

time: 21.5 us -> 19.4 us (0.902)
  Pallas kernels: 20.3 us -> 18.1 us
    pallas_call x1, Pallas kernels: 20.3 us -> 18.1 us  [kernel_body(): pl.pallas_call(functools.partial(kernel, parts, strips), out_shape=jax.Sh...]
where the time goes in v3:
time: 19.4 us; the launch traced here: 19.1 us
  Pallas kernels  18.1 us (93%)
  local copies, waits for them, and re-layouts  0.97 us (5%)
    pallas_call x1, Pallas kernels, kernel_body(): pl.pallas_call(functools.partial(kernel, parts, strips), out_shape=jax.Sh...  18.1 us
    unnamed x1, local copies, waits for them, and re-layouts  0.97 us

profile of v3, /device:TPU:0, one launch (start us, length us, event | category | flops | bytes accessed | tf_op | source)
XLA Modules:
  0.0 19.1 jit_solution(15997194399114557510)
XLA Ops:
  0.0 18.1 %sar.1 = f32[16,32,512]{2,1,0:T(8,128)S(1)} custom-call(s32[2]{0:T(128)} %offsets_hbm.1, bf16[2,128,2048]{2,1,0:T(8,128)(2,1)} %spectra_hbm.1, bf16[4,128,512]{2,1,0:T(8,128)(2,1)} %constant.6.clone.columns_hbm, bf16[256,640]{1,0:T(8,128)(2,1)} %constant.7.clone.rows_hbm, bf16[2,512,640]{2,1,0:T(8,128)(2,1)} %constant.8.clone.weights_hbm), custom_call_target="tpu_custom_call" | custom-call | tf_op jit(solution)/shard_map/sar/pallas_call | solution.py:397
  18.1 1.0 %copy.7 = f32[512,16,32]{0,2,1:T(8,128)} copy(f32[512,16,32]{0,2,1:T(8,128)S(1)} %bitcast.1) | data formatting | bytes 2097152

commit v4 on v3

--- a/solution.py
+++ b/solution.py
@@ -279,14 +279,17 @@
     kept.start()
 
     alternate = 1.0 - 2.0 * lax.rem(lax.broadcasted_iota(jnp.int32, (1, 1, 2 * depth), 2), 2).astype(jnp.float32)
-    signs = [1.0 - strip * (1.0 + alternate), 1.0 - strip * (1.0 - alternate)]
+
+    def sign_of(h):
+        return 1.0 - strip * (1.0 + (1 - 2 * h) * alternate)
+
     row_at = lax.broadcasted_iota(jnp.int32, (GROUP, 8, 2 * depth), 1)
 
     def window(h, first, count):
         block = []
         for step in range(count + 1):
             at = lax.rem(first + step, LAYERS) * GROUP
-            block.append(held[h, pl.ds(at, GROUP)].astype(jnp.float32) * signs[h][None])
+            block.append(held[h, pl.ds(at, GROUP)].astype(jnp.float32) * sign_of(h)[None])
         whole = jnp.concatenate(block, axis=0)
         number = count * GROUP
         body = whole[:, : 2 * RADIX].reshape(number + GROUP, 2 * width, 2 * depth)
@@ -314,9 +317,11 @@
     outside = ((tail == high) & (strip == strips - 1)) | ((tail == high + LANES - 1) & (strip == 0))
     inside = jnp.where(outside, 0.0, 1.0)
 
-    def image(lower_half, upper_half):
-        total = upper_half + lower_half
-        gap = upper_half - lower_half
+    facing = (2 * strip - 1).astype(jnp.float32)
+
+    def image(mine, theirs):
+        total = mine + theirs
+        gap = (mine - theirs) * facing
         size = total.shape[0]
         lhs[:size, :depth] = total[:, :depth].astype(jnp.bfloat16)
         lhs[:size, depth:] = gap[:, depth:].astype(jnp.bfloat16)
@@ -341,13 +346,13 @@
     for source in [me] + close:
         arrival(other, source, got_sem).wait_recv()
     loads[4].wait()
-    pieces = image(window(0, 2 * upper, 1), window(1, 2 * upper, 1))
+    pieces = image(window(strip, 2 * upper, 1), window(other, 2 * upper, 1))
     size = 2 * batch + 2 * 8
     for i, piece in enumerate(pieces):
         boxed[0, i * (size // 2) : (i + 1) * (size // 2)] = piece
     for source in origins[:GROUP]:
         arrival(other, source, got_sem).wait_recv()
-    pieces = image(window(0, LAYERS - 1, 1), window(1, LAYERS - 1, 1))
+    pieces = image(window(strip, LAYERS - 1, 1), window(other, LAYERS - 1, 1))
     for i, piece in enumerate(pieces):
         boxed[1, i * (size // 2) : (i + 1) * (size // 2)] = piece
     early = boxed[:, : 2 * batch].reshape(2, 2 * GROUP, width, high)
@@ -362,19 +367,31 @@
     level[top : top + 32] = (early_near - near_mean[None]).reshape(32, high).astype(jnp.bfloat16)
     level[top + 64 :] = jnp.zeros((level.shape[0] - top - 64, high), jnp.bfloat16)
 
+    loads[5].wait()
+    frames = 2 * parts
+    step = 16
+    for c in range(0, width, step):
+        piece = product_of(weights[c * frames : (c + step) * frames, : 4 * batch], level[: 4 * batch])
+        out_ref[c : c + step] = piece.reshape(step, frames, high)
+    mine = window(strip, 1 - upper, 2)
     for source in origins[GROUP:]:
         arrival(other, source, got_sem).wait_recv()
-    pieces = image(window(0, 1 - upper, 2), window(1, 1 - upper, 2))
+    pieces = image(mine, window(other, 1 - upper, 2))
     late = jnp.concatenate(pieces, axis=0)
     block = late[: 4 * batch].reshape(4 * GROUP, width, high)
     level[4 * batch : 8 * batch] = (block - mean[None]).reshape(4 * batch, high).astype(jnp.bfloat16)
-    near = late[4 * batch :].reshape(4, 8, high)
-    level[top + 32 : top + 64] = (near - near_mean[None]).reshape(32, high).astype(jnp.bfloat16)
-    loads[5].wait()
-    frames = 2 * parts
-    for c in range(0, width, 4):
-        piece = product_of(weights[c * frames : (c + 4) * frames], level[...])
-        out_ref[c : c + 4] = (piece * (1.0 / 9.0)).reshape(4, frames, high)
+    late_near = late[4 * batch :].reshape(4, 8, high)
+    level[top + 32 : top + 64] = (late_near - near_mean[None]).reshape(32, high).astype(jnp.bfloat16)
+    for c in range(0, width, step):
+        piece = product_of(weights[c * frames : (c + step) * frames, 4 * batch : 8 * batch], level[4 * batch : 8 * batch])
+        piece = out_ref[c : c + step] + piece.reshape(step, frames, high)
+        for edge_column in (0, width - 1):
+            if c <= edge_column < c + step:
+                extra = product_of(weights[edge_column * frames : (edge_column + 1) * frames, 8 * batch :], level[8 * batch :])
+                row = edge_column - c
+                parts_of = [piece[:row], piece[row : row + 1] + extra[None], piece[row + 1 :]]
+                piece = jnp.concatenate([part for part in parts_of if part.shape[0]], axis=0)
+        out_ref[c : c + step] = piece * (1.0 / 9.0)
     for to in targets + close:
         send(to).wait_send()
     for to in [me] + close:

time: 19.4 us -> 19 us (0.979)
  Pallas kernels: 18.1 us -> 17.7 us
    pallas_call x1, Pallas kernels: 18.1 us -> 17.7 us  [kernel_body(): pl.pallas_call(functools.partial(kernel, parts, strips), out_shape=jax.Sh...]
where the time goes in v4:
time: 19 us; the launch traced here: 18.7 us
  Pallas kernels  17.7 us (93%)
  local copies, waits for them, and re-layouts  0.97 us (5%)
    pallas_call x1, Pallas kernels, kernel_body(): pl.pallas_call(functools.partial(kernel, parts, strips), out_shape=jax.Sh...  17.7 us
    unnamed x1, local copies, waits for them, and re-layouts  0.97 us

profile of v4, /device:TPU:0, one launch (start us, length us, event | category | flops | bytes accessed | tf_op | source)
XLA Modules:
  0.0 18.7 jit_solution(16288495896768629141)
XLA Ops:
  0.0 17.7 %sar.1 = f32[16,32,512]{2,1,0:T(8,128)S(1)} custom-call(s32[2]{0:T(128)} %offsets_hbm.1, bf16[2,128,2048]{2,1,0:T(8,128)(2,1)} %spectra_hbm.1, bf16[4,128,512]{2,1,0:T(8,128)(2,1)} %constant.6.clone.columns_hbm, bf16[256,640]{1,0:T(8,128)(2,1)} %constant.7.clone.rows_hbm, bf16[2,512,640]{2,1,0:T(8,128)(2,1)} %constant.8.clone.weights_hbm), custom_call_target="tpu_custom_call" | custom-call | tf_op jit(solution)/shard_map/sar/pallas_call | solution.py:414
  17.7 1.0 %copy.7 = f32[512,16,32]{0,2,1:T(8,128)} copy(f32[512,16,32]{0,2,1:T(8,128)S(1)} %bitcast.1) | data formatting | bytes 2097152

commit v5 on v4

--- a/solution.py
+++ b/solution.py
@@ -152,7 +152,7 @@
 def kernel(
     parts, strips, offsets_hbm, spectra_hbm, columns_hbm, rows_hbm, weights_hbm, out_ref,
     offsets_ref, spectra, columns, rows, weights, mixed, ends, edge, main, held, lhs, boxed, level,
-    load_sem, own_sem, send_sem, recv_sem, pass_sem, got_sem,
+    load_sem, own_sem, send_sem, recv_sem, pass_sem, got_sem, entry_sem,
 ):
     me, strip = lax.axis_index("sub"), lax.axis_index("strip")
     width = COLS // parts
@@ -167,13 +167,23 @@
     def device_at(half, step, turn):
         return (half * reach + step) * GROUP + lax.rem(place + turn + GROUP, GROUP)
 
-    close = [device_at(upper, within, turn) for turn in range(1, GROUP)]
-    close += [
-        device_at(upper, lax.rem(within + step, reach), turn) for step in range(1, reach) for turn in range(GROUP)
-    ]
-    outward = [(1 - upper) * (reach - 1) + (2 * upper - 1) * step for step in range(reach)]
-    targets = [device_at(1 - upper, step, turn) for step in outward for turn in range(GROUP)]
-    origins = [device_at(1 - upper, step, -turn) for step in outward for turn in range(GROUP)]
+    def aside(step, shift, twist):
+        row, core = lax.rem(place // 2 + shift, 2), lax.rem(place + twist, 2)
+        return (upper * reach + lax.rem(within + step, reach)) * GROUP + 2 * row + core
+
+    beside = [aside(0, 0, 1), aside(0, 1, 0), aside(0, 1, 1)]
+    near = [aside(1, 0, 0), aside(1, 0, 1)]
+    diagonal = [aside(1, 1, 0), aside(1, 1, 1)]
+    close = beside + near + diagonal
+    opening = layer == reach
+    closing = layer == LAYERS - 1
+    skipped = 2 * len(diagonal) * (layer // reach) * (1 - lax.rem(layer, reach))
+    outward = [step for step in range(reach)]
+    targets = [device_at(1 - upper, outward[step], turn) for step, turn in [(0, 0), (0, 1), (0, 2), (0, 3), (1, 0), (1, 1), (1, 2), (1, 3)]]
+    waits = [(0, 0), (0, 1), (0, 2), (0, 3), (1, 0), (1, 1), (1, 2), (1, 3)]
+    origins = [device_at(1 - upper, (1 - upper) + (2 * upper - 1) * step, -turn) for step, turn in waits]
+    firsts = [device_at(1 - upper, 1 - upper, -turn) for turn in range(GROUP)]
+    lasts = [device_at(1 - upper, upper, -turn) for turn in range(GROUP)]
 
     def load(source, target, i):
         return pltpu.make_async_copy(source, target, load_sem.at[i])
@@ -189,17 +199,21 @@
     for copy in loads[:4]:
         copy.start()
     barrier = pltpu.get_barrier_semaphore()
-    for away in range(1, parts):
-        pl.semaphore_signal(barrier, inc=1, device_id=(lax.rem(me + away, parts), strip), device_id_type=MESH)
-    for near in [me] + close:
-        pl.semaphore_signal(barrier, inc=1, device_id=(near, other), device_id_type=MESH)
-
-    loads[0].wait()
-    lane = lax.broadcasted_iota(jnp.int32, (1, 2 * depth), 1)
-    sample = strip * depth + jnp.where(lane < depth, lane, lane - depth) - KR // 2
-    offset = jnp.where(lane < depth, offsets_ref[0], offsets_ref[1])
-    angle = jnp.bitwise_and(offset * sample, ROWS - 1).astype(jnp.float32) * (2.0 * math.pi / ROWS)
-    cosine, sine = jnp.cos(angle), jnp.sin(angle)
+
+    def announce(to, side):
+        pl.semaphore_signal(barrier, inc=1, device_id=(to, side), device_id_type=MESH)
+
+    for to in targets + beside + near:
+        announce(to, strip)
+    for to in [me] + beside + near:
+        announce(to, other)
+
+    @pl.when(jnp.logical_not(closing))
+    def _():
+        for to in diagonal:
+            announce(to, strip)
+            announce(to, other)
+
     edge[...] = jnp.zeros_like(edge)
     quarter = samples // RADIX
     for own in range(2):
@@ -216,6 +230,12 @@
             for part, value in enumerate(pair):
                 mixed[residue, own * depth : (own + 1) * depth, part * quarter : (part + 1) * quarter] = value.astype(jnp.bfloat16)
     loads[3].wait()
+    loads[0].wait()
+    lane = lax.broadcasted_iota(jnp.int32, (1, 2 * depth), 1)
+    sample = strip * depth + jnp.where(lane < depth, lane, lane - depth) - KR // 2
+    offset = jnp.where(lane < depth, offsets_ref[0], offsets_ref[1])
+    angle = jnp.bitwise_and(offset * sample, ROWS - 1).astype(jnp.float32) * (2.0 * math.pi / ROWS)
+    cosine, sine = jnp.cos(angle), jnp.sin(angle)
     for copy in loads[4:]:
         copy.start()
     rank = COLS // RADIX
@@ -244,7 +264,7 @@
                 edge[d, 2 * own + 1 : 2 * own + 2] = ends[2 * own + 1, (d + 1) * slots : (d + 1) * slots + 1]
     main[:, 2 * RADIX] = edge[:, :4].astype(jnp.bfloat16)
 
-    pl.semaphore_wait(barrier, parts + len(close))
+    pl.semaphore_wait(barrier, parts + len(close) - skipped)
 
     def send(to):
         return pltpu.make_async_remote_copy(
@@ -270,13 +290,34 @@
             recv_sem=got_sem.at[source], device_id=(me, other), device_id_type=MESH,
         )
 
-    for to, near in zip(targets, [me] + close):
+    for index, to in enumerate(targets):
         send(to).start()
-        cross(near).start()
-    for to in close:
+        if index < len(close) - 1:
+            cross(([me] + beside + near)[index]).start()
+    for to in beside + near:
         send(to).start()
+
+    def send_diagonal():
+        for to in diagonal:
+            send(to).start()
+            cross(to).start()
+
+    pl.when(jnp.logical_not(opening))(send_diagonal)
+
+    @pl.when(closing)
+    def _():
+        for to in diagonal:
+            pl.semaphore_signal(entry_sem, inc=1, device_id=(to, strip), device_id_type=MESH)
+            pl.semaphore_signal(entry_sem, inc=1, device_id=(to, other), device_id_type=MESH)
+
     kept = pltpu.make_async_copy(main.at[me], held.at[strip, me], own_sem.at[0])
     kept.start()
+
+    @pl.when(opening)
+    def _():
+        pl.semaphore_wait(entry_sem, 2 * len(diagonal))
+        send_diagonal()
+
 
     alternate = 1.0 - 2.0 * lax.rem(lax.broadcasted_iota(jnp.int32, (1, 1, 2 * depth), 2), 2).astype(jnp.float32)
 
@@ -350,7 +391,7 @@
     size = 2 * batch + 2 * 8
     for i, piece in enumerate(pieces):
         boxed[0, i * (size // 2) : (i + 1) * (size // 2)] = piece
-    for source in origins[:GROUP]:
+    for source in firsts:
         arrival(other, source, got_sem).wait_recv()
     pieces = image(window(strip, LAYERS - 1, 1), window(other, LAYERS - 1, 1))
     for i, piece in enumerate(pieces):
@@ -374,7 +415,7 @@
         piece = product_of(weights[c * frames : (c + step) * frames, : 4 * batch], level[: 4 * batch])
         out_ref[c : c + step] = piece.reshape(step, frames, high)
     mine = window(strip, 1 - upper, 2)
-    for source in origins[GROUP:]:
+    for source in lasts:
         arrival(other, source, got_sem).wait_recv()
     pieces = image(mine, window(other, 1 - upper, 2))
     late = jnp.concatenate(pieces, axis=0)
@@ -433,6 +474,7 @@
             pltpu.SemaphoreType.DMA((parts,)),
             pltpu.SemaphoreType.DMA((parts,)),
             pltpu.SemaphoreType.DMA((parts,)),
+            pltpu.SemaphoreType.REGULAR,
         ],
         compiler_params=pltpu.CompilerParams(collective_id=0, has_side_effects=True, vmem_limit_bytes=48 << 20),
         name="sar",

time: 19 us -> 18.8 us (0.989); the launches traced: 18.7 us -> 18.7 us
  no operation moved by 1% of the time
where the time goes in v5:
time: 18.8 us; the launch traced here: 18.7 us
  Pallas kernels  17.7 us (94%)
  local copies, waits for them, and re-layouts  0.97 us (5%)
    pallas_call x1, Pallas kernels, kernel_body(): pl.pallas_call(functools.partial(kernel, parts, strips), out_shape=jax.Sh...  17.7 us
    unnamed x1, local copies, waits for them, and re-layouts  0.97 us

profile of v5, /device:TPU:0, one launch (start us, length us, event | category | flops | bytes accessed | tf_op | source)
XLA Modules:
  0.0 18.7 jit_solution(11849017704888044327)
XLA Ops:
  0.0 17.7 %sar.1 = f32[16,32,512]{2,1,0:T(8,128)S(1)} custom-call(s32[2]{0:T(128)} %offsets_hbm.1, bf16[2,128,2048]{2,1,0:T(8,128)(2,1)} %spectra_hbm.1, bf16[4,128,512]{2,1,0:T(8,128)(2,1)} %constant.6.clone.columns_hbm, bf16[256,640]{1,0:T(8,128)(2,1)} %constant.7.clone.rows_hbm, bf16[2,512,640]{2,1,0:T(8,128)(2,1)} %constant.8.clone.weights_hbm), custom_call_target="tpu_custom_call" | custom-call | tf_op jit(solution)/shard_map/sar/pallas_call | solution.py:455
  17.7 1.0 %copy.7 = f32[512,16,32]{0,2,1:T(8,128)} copy(f32[512,16,32]{0,2,1:T(8,128)S(1)} %bitcast.1) | data formatting | bytes 2097152

commit v6 on v5

--- a/solution.py
+++ b/solution.py
@@ -152,7 +152,7 @@
 def kernel(
     parts, strips, offsets_hbm, spectra_hbm, columns_hbm, rows_hbm, weights_hbm, out_ref,
     offsets_ref, spectra, columns, rows, weights, mixed, ends, edge, main, held, lhs, boxed, level,
-    load_sem, own_sem, send_sem, recv_sem, pass_sem, got_sem, entry_sem,
+    load_sem, own_sem, send_sem, recv_sem, got_sem, entry_sem,
 ):
     me, strip = lax.axis_index("sub"), lax.axis_index("strip")
     width = COLS // parts
@@ -182,21 +182,18 @@
     targets = [device_at(1 - upper, outward[step], turn) for step, turn in [(0, 0), (0, 1), (0, 2), (0, 3), (1, 0), (1, 1), (1, 2), (1, 3)]]
     waits = [(0, 0), (0, 1), (0, 2), (0, 3), (1, 0), (1, 1), (1, 2), (1, 3)]
     origins = [device_at(1 - upper, (1 - upper) + (2 * upper - 1) * step, -turn) for step, turn in waits]
-    firsts = [device_at(1 - upper, 1 - upper, -turn) for turn in range(GROUP)]
-    lasts = [device_at(1 - upper, upper, -turn) for turn in range(GROUP)]
 
     def load(source, target, i):
         return pltpu.make_async_copy(source, target, load_sem.at[i])
 
     loads = [
         load(offsets_hbm, offsets_ref, 0),
-        load(spectra_hbm.at[0], spectra.at[0], 1),
-        load(spectra_hbm.at[1], spectra.at[1], 2),
-        load(columns_hbm, columns, 3),
-        load(rows_hbm, rows, 4),
-        load(weights_hbm.at[upper], weights, 5),
+        load(spectra_hbm, spectra, 1),
+        load(columns_hbm, columns, 2),
+        load(rows_hbm, rows, 3),
+        load(weights_hbm.at[upper], weights, 4),
     ]
-    for copy in loads[:4]:
+    for copy in loads[:3]:
         copy.start()
     barrier = pltpu.get_barrier_semaphore()
 
@@ -216,8 +213,8 @@
 
     edge[...] = jnp.zeros_like(edge)
     quarter = samples // RADIX
+    loads[1].wait()
     for own in range(2):
-        loads[1 + own].wait()
         re = [spectra[own, :, p * quarter : (p + 1) * quarter].astype(jnp.float32) for p in range(RADIX)]
         im = [spectra[own, :, samples + p * quarter : samples + (p + 1) * quarter].astype(jnp.float32) for p in range(RADIX)]
         even_re, even_im, gap_re, gap_im = re[0] + re[2], im[0] + im[2], re[0] - re[2], im[0] - im[2]
@@ -229,14 +226,14 @@
         for residue, pair in enumerate(folded):
             for part, value in enumerate(pair):
                 mixed[residue, own * depth : (own + 1) * depth, part * quarter : (part + 1) * quarter] = value.astype(jnp.bfloat16)
-    loads[3].wait()
+    loads[2].wait()
     loads[0].wait()
     lane = lax.broadcasted_iota(jnp.int32, (1, 2 * depth), 1)
     sample = strip * depth + jnp.where(lane < depth, lane, lane - depth) - KR // 2
     offset = jnp.where(lane < depth, offsets_ref[0], offsets_ref[1])
     angle = jnp.bitwise_and(offset * sample, ROWS - 1).astype(jnp.float32) * (2.0 * math.pi / ROWS)
     cosine, sine = jnp.cos(angle), jnp.sin(angle)
-    for copy in loads[4:]:
+    for copy in loads[3:]:
         copy.start()
     rank = COLS // RADIX
     slots = width // RADIX
@@ -266,32 +263,33 @@
 
     pl.semaphore_wait(barrier, parts + len(close) - skipped)
 
+    def remote(source, h, to, side, sent, landed):
+        return pltpu.make_async_remote_copy(
+            src_ref=source, dst_ref=held.at[strip, h], send_sem=sent, recv_sem=landed,
+            device_id=(to, side), device_id_type=MESH,
+        )
+
     def send(to):
-        return pltpu.make_async_remote_copy(
-            src_ref=main.at[to], dst_ref=held.at[strip, me], send_sem=send_sem.at[to],
-            recv_sem=recv_sem.at[me], device_id=(to, strip), device_id_type=MESH,
-        )
-
-    def arrival(h, source, sem):
-        return pltpu.make_async_remote_copy(
-            src_ref=main.at[source], dst_ref=held.at[h, source], send_sem=send_sem.at[source],
-            recv_sem=sem.at[source], device_id=(source, strip), device_id_type=MESH,
-        )
+        return remote(main.at[to], me, to, strip, send_sem.at[0], recv_sem.at[parts // 2])
+
+    def send_far(to):
+        return remote(main.at[to], me, to, strip, send_sem.at[0], recv_sem.at[lax.rem(me, parts // 2)])
 
     def cross(to):
-        return pltpu.make_async_remote_copy(
-            src_ref=main.at[to], dst_ref=held.at[strip, me], send_sem=pass_sem.at[to],
-            recv_sem=got_sem.at[me], device_id=(to, other), device_id_type=MESH,
-        )
-
-    def forward(source):
-        return pltpu.make_async_remote_copy(
-            src_ref=held.at[strip, source], dst_ref=held.at[strip, source], send_sem=pass_sem.at[source],
-            recv_sem=got_sem.at[source], device_id=(me, other), device_id_type=MESH,
-        )
+        return remote(main.at[to], me, to, other, send_sem.at[1], got_sem.at[0])
+
+    def forward(source, group):
+        return remote(held.at[strip, source], source, me, other, send_sem.at[1], got_sem.at[1 + group])
+
+    def far_arrival(source):
+        sem = recv_sem.at[lax.rem(source, parts // 2)]
+        return pltpu.make_async_copy(main.at[source], held.at[strip, source], sem)
+
+    def together(h, number, sem):
+        return pltpu.make_async_copy(main.at[pl.ds(0, number)], held.at[h, pl.ds(0, number)], sem)
 
     for index, to in enumerate(targets):
-        send(to).start()
+        send_far(to).start()
         if index < len(close) - 1:
             cross(([me] + beside + near)[index]).start()
     for to in beside + near:
@@ -378,21 +376,18 @@
         return pieces
 
     batch = GROUP * width
-    for source in origins:
-        arrival(strip, source, recv_sem).wait_recv()
-        forward(source).start()
-    for source in close:
-        arrival(strip, source, recv_sem).wait_recv()
+    for index, source in enumerate(origins):
+        far_arrival(source).wait()
+        forward(source, index // GROUP).start()
+    together(strip, len(close), recv_sem.at[parts // 2]).wait()
     kept.wait()
-    for source in [me] + close:
-        arrival(other, source, got_sem).wait_recv()
-    loads[4].wait()
+    together(other, parts // 2, got_sem.at[0]).wait()
+    loads[3].wait()
     pieces = image(window(strip, 2 * upper, 1), window(other, 2 * upper, 1))
     size = 2 * batch + 2 * 8
     for i, piece in enumerate(pieces):
         boxed[0, i * (size // 2) : (i + 1) * (size // 2)] = piece
-    for source in firsts:
-        arrival(other, source, got_sem).wait_recv()
+    together(other, GROUP, got_sem.at[1]).wait()
     pieces = image(window(strip, LAYERS - 1, 1), window(other, LAYERS - 1, 1))
     for i, piece in enumerate(pieces):
         boxed[1, i * (size // 2) : (i + 1) * (size // 2)] = piece
@@ -408,15 +403,14 @@
     level[top : top + 32] = (early_near - near_mean[None]).reshape(32, high).astype(jnp.bfloat16)
     level[top + 64 :] = jnp.zeros((level.shape[0] - top - 64, high), jnp.bfloat16)
 
-    loads[5].wait()
+    loads[4].wait()
     frames = 2 * parts
     step = 16
     for c in range(0, width, step):
         piece = product_of(weights[c * frames : (c + step) * frames, : 4 * batch], level[: 4 * batch])
         out_ref[c : c + step] = piece.reshape(step, frames, high)
     mine = window(strip, 1 - upper, 2)
-    for source in lasts:
-        arrival(other, source, got_sem).wait_recv()
+    together(other, GROUP, got_sem.at[2]).wait()
     pieces = image(mine, window(other, 1 - upper, 2))
     late = jnp.concatenate(pieces, axis=0)
     block = late[: 4 * batch].reshape(4 * GROUP, width, high)
@@ -433,12 +427,8 @@
                 parts_of = [piece[:row], piece[row : row + 1] + extra[None], piece[row + 1 :]]
                 piece = jnp.concatenate([part for part in parts_of if part.shape[0]], axis=0)
         out_ref[c : c + step] = piece * (1.0 / 9.0)
-    for to in targets + close:
-        send(to).wait_send()
-    for to in [me] + close:
-        cross(to).wait_send()
-    for source in origins:
-        forward(source).wait_send()
+    together(strip, parts - 1, send_sem.at[0]).wait()
+    together(strip, parts, send_sem.at[1]).wait()
 
 
 def kernel_body(spectra, offsets):
@@ -468,12 +458,11 @@
             pltpu.VMEM((4 * half, KR), bf16),
             pltpu.VMEM((2, half, high), f32),
             pltpu.VMEM((padded, high), bf16),
-            pltpu.SemaphoreType.DMA((6,)),
+            pltpu.SemaphoreType.DMA((5,)),
             pltpu.SemaphoreType.DMA((1,)),
-            pltpu.SemaphoreType.DMA((parts,)),
-            pltpu.SemaphoreType.DMA((parts,)),
-            pltpu.SemaphoreType.DMA((parts,)),
-            pltpu.SemaphoreType.DMA((parts,)),
+            pltpu.SemaphoreType.DMA((2,)),
+            pltpu.SemaphoreType.DMA((parts // 2 + 1,)),
+            pltpu.SemaphoreType.DMA((3,)),
             pltpu.SemaphoreType.REGULAR,
         ],
         compiler_params=pltpu.CompilerParams(collective_id=0, has_side_effects=True, vmem_limit_bytes=48 << 20),

time: 18.8 us -> 18.6 us (0.989)
  Pallas kernels: 17.7 us -> 17.5 us
    pallas_call x1, Pallas kernels: 17.7 us -> 17.5 us  [kernel_body(): pl.pallas_call(functools.partial(kernel, parts, strips), out_shape=jax.Sh...]
where the time goes in v6:
time: 18.6 us; the launch traced here: 18.4 us
  Pallas kernels  17.5 us (94%)
  local copies, waits for them, and re-layouts  0.97 us (5%)
    pallas_call x1, Pallas kernels, kernel_body(): pl.pallas_call(functools.partial(kernel, parts, strips), out_shape=jax.Sh...  17.5 us
    unnamed x1, local copies, waits for them, and re-layouts  0.97 us

profile of v6, /device:TPU:0, one launch (start us, length us, event | category | flops | bytes accessed | tf_op | source)
XLA Modules:
  0.0 18.4 jit_solution(5852702112670477101)
XLA Ops:
  0.0 17.5 %sar.1 = f32[16,32,512]{2,1,0:T(8,128)S(1)} custom-call(s32[2]{0:T(128)} %offsets_hbm.1, bf16[2,128,2048]{2,1,0:T(8,128)(2,1)} %spectra_hbm.1, bf16[4,128,512]{2,1,0:T(8,128)(2,1)} %constant.6.clone.columns_hbm, bf16[256,640]{1,0:T(8,128)(2,1)} %constant.7.clone.rows_hbm, bf16[2,512,640]{2,1,0:T(8,128)(2,1)} %constant.8.clone.weights_hbm), custom_call_target="tpu_custom_call" | custom-call | tf_op jit(solution)/shard_map/sar/pallas_call | solution.py:445
  17.5 1.0 %copy.7 = f32[512,16,32]{0,2,1:T(8,128)} copy(f32[512,16,32]{0,2,1:T(8,128)S(1)} %bitcast.1) | data formatting | bytes 2097152
